TPU v7x, 256 devices: a whole 4x4x8 slice. The times are simulated.
256 devices in a mesh: il: 16 (over y, x), xl: 16 (over z, core).
Axes of the slice: x: 4, y: 4, z: 8, core: 2. Of those that a mesh axis runs over, the one named last changes fastest.
Arguments:
- patches: bfloat16 [16, 192, 128, 768], P('il', 'xl'), may hold values from -9 to 9
- out_cot: bfloat16 [16, 192, 128, 768], P('il', 'xl'), may hold values from -6 to 6
- vis_count: int32 [16, 192], P('il', 'xl'), may hold values from 0 to 128, as said below
- w_qkv: bfloat16 [768, 1152], P(('il', 'xl')), may hold values from -1.5 to 1.5
- w_out: bfloat16 [768, 384], P(('il', 'xl')), may hold values from -0.3125 to 0.3125
- ln_gain: float32 [768], replicated, may hold values from 0.1 to 1.9
Outputs:
- enc_out: bfloat16 [16, 192, 128, 768], P('il', 'xl')
- grad_in: bfloat16 [16, 192, 128, 768], P('il', 'xl')
- grad_wqkv: float32 [768, 1152], P(('il', 'xl'))
- grad_wout: float32 [768, 384], P(('il', 'xl'))
Inputs may be any that keep to these rules, and one draw needn't show every extreme that they name: `vis_count`: A block with count 0 holds no data. On each inline row of tiles exactly 96 blocks have data; one device holds 0 to 12 of them, and some device of each row holds 12.
All inputs are finite; a program needn't handle non-finite values.
Results may differ from a plain program's by a relative error of at most 0.0096.
Values may be sent and summed in bfloat16 or wider, within the bound.
No kernel may reach another device: no remote copies, remote signals or barrier semaphores. Data moves between devices by JAX's collectives and lax.ppermute only.
A program may use at most 128 MiB of HBM per device.

v0:
```python
import jax
import jax.numpy as jnp
from jax import lax
from jax.sharding import PartitionSpec as P

HEAD_DIM = 64
HEADS = 6


def block_pass(tiles, cotan, counts, weights_qkv, weights_out, ln_gain):
    nblock, vrows, width = tiles.shape
    inner = HEADS * HEAD_DIM
    factor = HEAD_DIM ** (-0.5)
    positions = jnp.arange(vrows)
    row_mask = (positions[None, :] < counts[:, None]).astype(jnp.float32)
    tiles_f = tiles.astype(jnp.float32)
    centred = tiles_f - jnp.mean(tiles_f, axis=-1, keepdims=True)
    inv_std = lax.rsqrt(jnp.mean(centred * centred, axis=-1, keepdims=True) + 1e-06)
    normed = centred * inv_std
    normed_b = (normed * ln_gain).astype(jnp.bfloat16).reshape(nblock * vrows, width)
    project = jnp.dot(normed_b, weights_qkv, preferred_element_type=jnp.float32).astype(
        jnp.bfloat16
    )
    project = project.reshape(nblock, vrows, 3, HEADS, HEAD_DIM)
    queries = project[:, :, 0]
    keys_b = project[:, :, 1]
    values_b = project[:, :, 2]
    scores = (
        jnp.einsum("nqhe,nkhe->nhqk", queries, keys_b, preferred_element_type=jnp.float32) * factor
    )
    key_mask = (positions[None, :] < counts[:, None])[:, None, None, :]
    scores = jnp.where(key_mask, scores, jnp.float32(-1e30))
    probs_f = jnp.exp(scores - jnp.max(scores, axis=-1, keepdims=True))
    probs_f = probs_f / jnp.sum(probs_f, axis=-1, keepdims=True)
    probs_b = probs_f.astype(jnp.bfloat16)
    attended = jnp.einsum("nhqk,nkhe->nqhe", probs_b, values_b, preferred_element_type=jnp.float32)
    attended = attended.astype(jnp.bfloat16).reshape(nblock * vrows, inner)
    mixed = lax.dot_general(
        attended, weights_out, (((1,), (1,)), ((), ())), preferred_element_type=jnp.float32
    )
    mixed = mixed.reshape(nblock, vrows, width)
    encoded = ((tiles_f + mixed) * row_mask[..., None]).astype(jnp.bfloat16)
    grad_out = (cotan * row_mask[..., None].astype(jnp.bfloat16)).reshape(nblock * vrows, width)
    grad_wout = lax.dot_general(
        grad_out, attended, (((0,), (0,)), ((), ())), preferred_element_type=jnp.float32
    )
    grad_att = jnp.dot(grad_out, weights_out, preferred_element_type=jnp.float32).astype(
        jnp.bfloat16
    )
    grad_att = grad_att.reshape(nblock, vrows, HEADS, HEAD_DIM)
    grad_prob = jnp.einsum(
        "nqhe,nkhe->nhqk", grad_att, values_b, preferred_element_type=jnp.float32
    )
    grad_val = jnp.einsum("nhqk,nqhe->nkhe", probs_b, grad_att, preferred_element_type=jnp.float32)
    grad_score = (
        probs_f * (grad_prob - jnp.sum(probs_f * grad_prob, axis=-1, keepdims=True)) * factor
    )
    grad_score = grad_score.astype(jnp.bfloat16)
    grad_query = jnp.einsum(
        "nhqk,nkhe->nqhe", grad_score, keys_b, preferred_element_type=jnp.float32
    )
    grad_key = jnp.einsum(
        "nhqk,nqhe->nkhe", grad_score, queries, preferred_element_type=jnp.float32
    )
    grad_proj = (
        jnp.stack([grad_query, grad_key, grad_val], axis=2)
        .astype(jnp.bfloat16)
        .reshape(nblock * vrows, 3 * inner)
    )
    grad_wqkv = lax.dot_general(
        normed_b, grad_proj, (((0,), (0,)), ((), ())), preferred_element_type=jnp.float32
    )
    grad_norm = lax.dot_general(
        grad_proj, weights_qkv, (((1,), (1,)), ((), ())), preferred_element_type=jnp.float32
    )
    grad_norm = grad_norm.reshape(nblock, vrows, width) * ln_gain
    grad_ln = inv_std * (
        grad_norm
        - jnp.mean(grad_norm, axis=-1, keepdims=True)
        - normed * jnp.mean(grad_norm * normed, axis=-1, keepdims=True)
    )
    grad_rows = grad_out.reshape(nblock, vrows, width).astype(jnp.float32)
    grad_input = ((grad_rows + grad_ln) * row_mask[..., None]).astype(jnp.bfloat16)
    return (encoded, grad_input, grad_wqkv, grad_wout)


def shards(patches, out_cot, vis_count, w_qkv, w_out, ln_gain):
    full_qkv, full_out = (
        lax.all_gather(w_qkv, ("il", "xl"), axis=0, tiled=True),
        lax.all_gather(w_out, ("il", "xl"), axis=0, tiled=True),
    )
    tiles = patches[0]
    cotan = out_cot[0]
    counts = vis_count[0]
    encoded, grad_input, grad_qkv, grad_proj_out = block_pass(
        tiles, cotan, counts, full_qkv, full_out, ln_gain
    )
    grad_terms = jnp.concatenate([grad_qkv, grad_proj_out], axis=1)
    summed = lax.psum_scatter(grad_terms, ("il", "xl"), scatter_dimension=0, tiled=True)
    qkv_width = grad_qkv.shape[1]
    return (encoded[None], grad_input[None], summed[:, :qkv_width], summed[:, qkv_width:])


def solution(mesh):
    return jax.shard_map(
        shards,
        mesh=mesh,
        in_specs=(
            P("il", "xl", None, None),
            P("il", "xl", None, None),
            P("il", "xl"),
            P(("il", "xl"), None),
            P(("il", "xl"), None),
            P(),
        ),
        out_specs=(
            P("il", "xl", None, None),
            P("il", "xl", None, None),
            P(("il", "xl"), None),
            P(("il", "xl"), None),
        ),
        check_vma=False,
    )
```

profile of v0, /device:TPU:2, one launch (start us, length us, event | category | flops | bytes accessed | tf_op | source)
XLA Modules:
  0.0 488.9 jit_solution(13470428343686679741)
XLA Ops:
  7.2 0.0 all-gather.4.cloned.1.call-start
  7.2 0.7 all-gather.4.cloned.1.call-update
  7.9 0.0 all-reduce.3.cloned.1.call-start
  7.9 77.2 %all-gather.1 = bf16[256,3,384]{2,1,0:T(4,128)(2,1)S(1)} all-gather(bf16[1,3,384]{2,1,0:T(4,128)(2,1)} %bitcast.129), channel_id=1, replica_groups=mesh['il'=16,'xl'=16] {'il','xl'}, dimensions={0}, use_global_device_ids=true | all-gather | bytes 592128 | tf_op jit(solution)/shard_map/all_gather | solution.py:90
  85.2 1.2 reshape.185
  86.4 0.8 convert_convert_fusion
  87.2 1.9 bitcast_multiply_fusion
  89.1 2.4 convolution_convert_fusion.1
  91.6 4.8 reshape.191
  96.4 4.2 copy.45
  100.6 0.4 convert_reduce_fusion
  101.0 0.8 fusion.15
  101.8 0.4 copy-done.2
  102.3 1.7 broadcast_multiply_fusion
  104.0 1.9 fusion.18
  105.9 2.0 fusion.4
  107.9 11.0 %all-gather.4.cloned.1.call-done = bf16[256,3,1152]{2,1,0:T(4,128)(2,1)} async-done(((bf16[1,3,1152]{2,1,0:T(4,128)(2,1)}), bf16[256,3,1152]{2,1,0:T(4,128)(2,1)}) %all-gather.4.cloned.1.call-update) | async-done | bytes 1769488 | tf_op jit(solution)/shard_map/all_gather | solution.py:89
  118.8 5.2 %reshape.183 = bf16[768,1152]{1,0:T(8,128)(2,1)} reshape(bf16[256,3,1152]{2,1,0:T(4,128)(2,1)} %all-gather.4.cloned.1.call-done) | data formatting | bytes 3538944
  124.0 7.2 %convolution_convert_fusion = bf16[1536,1152]{1,0:T(8,128)(2,1)} fusion(bf16[1536,768]{1,0:T(8,128)(2,1)} %fusion.4, bf16[768,1152]{1,0:T(8,128)(2,1)} %reshape.183), kind=kOutput, calls=%fused_computation.2 | convolution fusion | flops 2719678464 | bytes 7667712 | tf_op jit(solution)/shard_map/dot_general | solution.py:21
  131.2 11.5 %reshape.190 = bf16[12,128,3,6,64]{4,3,2,1,0:T(8,128)(2,1)} reshape(bf16[1536,1152]{1,0:T(8,128)(2,1)} %convolution_convert_fusion) | data formatting | bytes 7077888 | tf_op jit(solution)/shard_map/reshape | solution.py:24
  142.7 6.5 %fusion.70 = (bf16[12,128,1,6,64]{4,3,2,1,0:T(8,128)(2,1)}, bf16[12,128,1,6,64]{4,3,2,1,0:T(8,128)(2,1)}, bf16[12,128,1,6,64]{4,3,2,1,0:T(8,128)(2,1)}) fusion(bf16[12,128,3,6,64]{4,3,2,1,0:T(8,128)(2,1)} %reshape.190), kind=kLoop, calls=%fused_computation.87 | loop fusion | bytes 7077888 | tf_op jit(solution)/shard_map/slice | solution.py:25
  149.2 4.2 copy.66
  153.4 4.2 copy.68
  157.7 4.2 copy.67
  161.9 2.5 fusion.51
  164.4 2.7 fusion.71
  167.2 1.8 convolution_convert_fusion.2
  169.0 0.7 copy-done.14
  169.6 2.8 convolution_bitcast_fusion
  172.4 3.0 fusion.55
  175.4 9.3 %fusion.44 = bf16[12,128,1,6,64]{1,4,3,0,2:T(8,128)(2,1)} fusion(f32[12,6,128,128]{2,3,1,0:T(8,128)} %fusion.55, bf16[12,128,1,6,64]{1,4,3,0,2:T(8,128)(2,1)} %copy.67, f32[12,6,128,128]{2,3,1,0:T(8,128)} %copy-done.14, f32[12,6,128]{2,1,0:T(8,128)S(1)} %get-tuple-element.17), kind=kOutput, calls=%fused_computation.53 | convolution fusion | flops 159261824 | bytes 11833344 | tf_op jit(solution)/shard_map/nhqk,nqhe->nkhe/dot_general | solution.py:62
  184.7 9.4 %fusion.41 = bf16[12,128,1,6,64]{1,4,3,0,2:T(8,128)(2,1)} fusion(f32[12,6,128,128]{2,3,1,0:T(8,128)} %fusion.55, bf16[12,128,1,6,64]{1,4,3,0,2:T(8,128)(2,1)} %copy.68, f32[12,6,128,128]{2,3,1,0:T(8,128)} %copy-done.14, f32[12,6,128]{2,1,0:T(8,128)S(1)} %get-tuple-element.17), kind=kOutput, calls=%fused_computation.52 | convolution fusion | flops 159261824 | bytes 11833344 | tf_op jit(solution)/shard_map/nhqk,nkhe->nqhe/dot_general | solution.py:59
  194.1 2.2 copy.53
  196.3 1.7 maximum_convert_fusion
  198.0 3.1 copy.52
  201.2 1.4 fusion.47
  202.6 0.2 copy-done.6
  202.8 3.3 fusion.23
  206.1 2.8 pad_maximum_fusion
  208.9 1.2 reshape.186
  210.2 5.1 %copy.50 = bf16[12,128,3,6,64]{1,4,3,2,0:T(8,128)(2,1)} copy(bf16[12,128,3,6,64]{1,4,3,0,2:T(8,128)(2,1)} %copy-done.1) | data formatting | bytes 7077888 | tf_op jit(solution)/shard_map/convert_element_type | solution.py:67
  215.2 5.2 %reshape.187 = bf16[768,1152,1]{1,0,2:T(8,128)(2,1)} reshape(bf16[256,3,1152]{2,1,0:T(4,128)(2,1)} %all-gather.4.cloned.1.call-done) | data formatting | bytes 3538944
  220.4 6.9 %multiply_reduce_fusion.1 = (f32[12,128]{1,0:T(8,128)S(1)}, f32[12,128]{1,0:T(8,128)S(1)}, f32[12,128,768]{2,1,0:T(8,128)S(1)}) fusion(f32[768]{0:T(1024)S(1)} %copy-done.13, f32[12,128]{1,0:T(8,128)S(1)} %get-tuple-element.9, f32[12,128]{1,0:T(8,128)S(1)} %get-tuple-element.12, bf16[1,12,128,768]{3,2,1,0:T(8,128)(2,1)S(1)} %copy-done, ...), kind=kOutput, calls=%fused_computation.34 | convolution fusion | flops 2726163456 | bytes 12413952 | tf_op jit(solution)/shard_map/dot_general | solution.py:73
  227.4 3.0 fusion.34
  230.4 3.4 fusion.39
  233.8 245.4 %all-reduce.3.cloned.1.call-done = f32[768,1536]{1,0:T(8,128)} async-done(((f32[768,1536]{1,0:T(8,128)}), f32[768,1536]{1,0:T(8,128)}) %all-reduce.3.cloned.1.call-update) | async-done | bytes 4718608
  479.2 1.5 constant_dynamic-slice_fusion
  480.7 1.4 dynamic-slice.2
  (31 shorter events, 0.1 us)
Async XLA Ops:
  7.2 111.6 %all-gather.4.cloned.1.call-start = ((), (), s32[]{:S(2)}) async-start(), calls=%async_computation | async-start | bytes 2368512 | tf_op jit(solution)/shard_map/all_gather | solution.py:89
  7.9 471.3 %all-reduce.3.cloned.1.call-start = ((), (), s32[]{:S(2)}) async-start(), calls=%async_computation.1 | async-start | bytes 9437184
  86.4 2.7 copy-start.12
  91.6 9.0 %copy-start = (bf16[1,12,128,768]{3,2,1,0:T(8,128)(2,1)S(1)}, bf16[1,12,128,768]{3,2,1,0:T(8,128)(2,1)}, u32[]{:S(2)}) copy-start(bf16[1,12,128,768]{3,2,1,0:T(8,128)(2,1)} %param.6) | copy-start | bytes 7077892
  100.6 1.7 copy-start.2
  101.0 3.0 copy-start.13
  164.4 2.8 copy-start.5
  167.1 2.5 copy-start.14
  167.2 2.5 copy-start.4
  194.0 2.2 copy-start.8
  194.1 2.3 copy-start.9
  198.0 3.1 copy-start.1
  198.0 3.1 copy-start.7
  201.2 1.7 copy-start.6
  220.4 7.0 %copy-start.10 = (bf16[12,6,64,128]{3,2,1,0:T(8,128)(2,1)S(1)}, bf16[12,6,64,128]{3,2,1,0:T(8,128)(2,1)}, u32[]{:S(2)}) copy-start(bf16[12,6,64,128]{3,2,1,0:T(8,128)(2,1)} %convolution_convert_fusion.2) | copy-start | bytes 3538948
  220.4 7.0 %copy-start.11 = (bf16[768,384,1]{1,0,2:T(8,128)(2,1)S(1)}, bf16[768,384,1]{1,0,2:T(8,128)(2,1)}, u32[]{:S(2)}) copy-start(bf16[768,384,1]{1,0,2:T(8,128)(2,1)} %reshape.186) | copy-start | bytes 1769476
  227.4 3.0 copy-start.3
Sparse Core Ops, SparseCore 0:
  11.6 107.2 all-gather.3
  209.0 270.0 all-reduce.2
where the time goes:
time: 490 us; the launch traced here: 489 us
  waiting for transfers between devices  257 us (52%)
  blocking collectives  77.2 us (16%)
  local copies, waits for them, and re-layouts  67.3 us (14%)
  matrix products  52.9 us (11%)
  other arithmetic  20.1 us (4%)
  between operations  14.3 us (3%)
    unnamed x3, waiting for transfers between devices  246 us
    all_gather x1, blocking collectives, shards(): lax.all_gather(w_out, ('il', 'xl'), axis=0, tiled=True)  77.2 us
    unnamed x37, local copies, waits for them, and re-layouts  27 us
    reshape x1, local copies, waits for them, and re-layouts, block_pass(): project = project.reshape(nblock, vrows, 3, HEADS, HEAD_DIM)  11.5 us
    all_gather x1, waiting for transfers between devices, shards(): lax.all_gather(w_qkv, ('il', 'xl'), axis=0, tiled=True)  11 us
  transfers between devices with their start and end apart: 2, of which 2 were waited for; matrix products, arithmetic and copies ran while one was open for 10% of the time, Pallas kernels for 0%

commit v1 on v0

--- a/solution.py
+++ b/solution.py
@@ -5,6 +5,11 @@
 
 HEAD_DIM = 64
 HEADS = 6
+
+
+def swapped_in(shard, axis, along):
+    outgoing = jnp.stack([shard] * lax.axis_size(axis))
+    return jnp.concatenate(lax.all_to_all(outgoing, axis, 0, 0), axis=along)
 
 
 def block_pass(tiles, cotan, counts, weights_qkv, weights_out, ln_gain):
@@ -87,7 +92,7 @@
 def shards(patches, out_cot, vis_count, w_qkv, w_out, ln_gain):
     full_qkv, full_out = (
         lax.all_gather(w_qkv, ("il", "xl"), axis=0, tiled=True),
-        lax.all_gather(w_out, ("il", "xl"), axis=0, tiled=True),
+        swapped_in(w_out, ("il", "xl"), 0),
     )
     tiles = patches[0]
     cotan = out_cot[0]

time: 490 us -> 492 us (level)
  blocking collectives: 77.2 us -> 0 us
  waiting for transfers between devices: 257 us -> 320 us
  starting transfers between devices: 0.08 us -> 14.8 us
    all_gather x1 -> x0, blocking collectives: 77.2 us -> none  [shards(): lax.all_gather(w_out, ('il', 'xl'), axis=0, tiled=True)]
    all_gather x1, waiting for transfers between devices: 11 us -> 56 us  [shards(): lax.all_gather(w_qkv, ('il', 'xl'), axis=0, tiled=True)]
    all_to_all x0 -> x1, waiting for transfers between devices: none -> 17.5 us  [swapped_in(): return jnp.concatenate(lax.all_to_all(outgoing, axis, 0, 0), axis=along)]
    all_to_all x0 -> x1, starting transfers between devices: none -> 14.7 us  [swapped_in(): return jnp.concatenate(lax.all_to_all(outgoing, axis, 0, 0), axis=along)]
    unnamed x37 -> x33, local copies, waits for them, and re-layouts: 27 us -> 23.9 us
  transfers between devices with their start and end apart: 2 -> 3, of which waited for: 2 -> 3; matrix products, arithmetic and copies ran while one was open for 10% -> 10% of each run, Pallas kernels for 0% -> 0%
where the time goes in v1:
time: 492 us; the launch traced here: 491 us
  waiting for transfers between devices  320 us (65%)
  local copies, waits for them, and re-layouts  68.1 us (14%)
  matrix products  56.3 us (11%)
  other arithmetic  17.3 us (4%)
  starting transfers between devices  14.8 us (3%)
  between operations  14.3 us (3%)
    unnamed x3, waiting for transfers between devices  246 us
    all_gather x1, waiting for transfers between devices, shards(): lax.all_gather(w_qkv, ('il', 'xl'), axis=0, tiled=True)  56 us
    unnamed x33, local copies, waits for them, and re-layouts  23.9 us
    all_to_all x1, waiting for transfers between devices, swapped_in(): return jnp.concatenate(lax.all_to_all(outgoing, axis, 0, 0), axis=along)  17.5 us
    all_to_all x1, starting transfers between devices, swapped_in(): return jnp.concatenate(lax.all_to_all(outgoing, axis, 0, 0), axis=along)  14.7 us
    reshape x1, local copies, waits for them, and re-layouts, block_pass(): project = project.reshape(nblock, vrows, 3, HEADS, HEAD_DIM)  11.5 us
  transfers between devices with their start and end apart: 3, of which 3 were waited for; matrix products, arithmetic and copies ran while one was open for 10% of the time, Pallas kernels for 0%

profile of v1, /device:TPU:2, one launch (start us, length us, event | category | flops | bytes accessed | tf_op | source)
XLA Modules:
  0.0 490.6 jit_solution(8502589810454640752)
XLA Ops:
  7.2 0.0 all-gather.3.cloned.1.call-start
  7.2 0.7 all-gather.3.cloned.1.call-update
  7.9 1.8 stack.10
  9.7 14.7 %all-to-all-start = ((bf16[256,3,384]{2,1,0:T(4,128)(2,1)}), bf16[256,3,384]{2,1,0:T(4,128)(2,1)S(1)}, u32[]{:S(2)}, u32[]{:S(2)}) async-start(bf16[256,3,384]{2,1,0:T(4,128)(2,1)} %stack.10), calls=%async_computation | async-start | bytes 1572864 | tf_op jit(solution)/shard_map/all_to_all | solution.py:12
  24.4 0.0 all-reduce.3.cloned.1.call-start
  24.4 0.9 convert_convert_fusion
  25.3 0.4 convert_reduce_fusion
  25.7 0.8 fusion.15
  26.6 1.7 broadcast_multiply_fusion
  28.3 1.9 fusion.18
  30.2 2.0 fusion.4
  32.2 17.5 %all-to-all-done = bf16[256,3,384]{2,1,0:T(4,128)(2,1)S(1)} async-done(((bf16[256,3,384]{2,1,0:T(4,128)(2,1)}), bf16[256,3,384]{2,1,0:T(4,128)(2,1)S(1)}, u32[]{:S(2)}, u32[]{:S(2)}) %all-to-all-start) | async-done | bytes 589856 | tf_op jit(solution)/shard_map/all_to_all | solution.py:12
  49.7 1.2 reshape.187
  50.9 4.2 convolution_convert_fusion.1
  55.1 4.7 reshape.198
  59.8 4.2 copy.45
  64.0 56.0 %all-gather.3.cloned.1.call-done = bf16[256,3,1152]{2,1,0:T(4,128)(2,1)} async-done(((bf16[1,3,1152]{2,1,0:T(4,128)(2,1)}), bf16[256,3,1152]{2,1,0:T(4,128)(2,1)}) %all-gather.3.cloned.1.call-update) | async-done | bytes 1769488 | tf_op jit(solution)/shard_map/all_gather | solution.py:94
  120.0 5.2 %reshape.192 = bf16[768,1152]{1,0:T(8,128)(2,1)} reshape(bf16[256,3,1152]{2,1,0:T(4,128)(2,1)} %all-gather.3.cloned.1.call-done) | data formatting | bytes 3538944
  125.2 7.2 %convolution_convert_fusion = bf16[1536,1152]{1,0:T(8,128)(2,1)} fusion(bf16[1536,768]{1,0:T(8,128)(2,1)} %fusion.4, bf16[768,1152]{1,0:T(8,128)(2,1)} %reshape.192), kind=kOutput, calls=%fused_computation.2 | convolution fusion | flops 2719678464 | bytes 7667712 | tf_op jit(solution)/shard_map/dot_general | solution.py:26
  132.4 11.5 %reshape.197 = bf16[12,128,3,6,64]{4,3,2,1,0:T(8,128)(2,1)} reshape(bf16[1536,1152]{1,0:T(8,128)(2,1)} %convolution_convert_fusion) | data formatting | bytes 7077888 | tf_op jit(solution)/shard_map/reshape | solution.py:29
  143.9 6.5 %fusion.69 = (bf16[12,128,1,6,64]{4,3,2,1,0:T(8,128)(2,1)}, bf16[12,128,1,6,64]{4,3,2,1,0:T(8,128)(2,1)}, bf16[12,128,1,6,64]{4,3,2,1,0:T(8,128)(2,1)}) fusion(bf16[12,128,3,6,64]{4,3,2,1,0:T(8,128)(2,1)} %reshape.197), kind=kLoop, calls=%fused_computation.85 | loop fusion | bytes 7077888 | tf_op jit(solution)/shard_map/slice | solution.py:30
  150.4 4.2 copy.66
  154.6 4.2 copy.68
  158.8 4.3 copy.67
  163.1 2.5 fusion.51
  165.6 2.7 fusion.70
  168.3 1.8 convolution_convert_fusion.2
  170.1 0.7 copy-done.13
  170.8 2.8 convolution_bitcast_fusion
  173.6 3.0 fusion.55
  176.6 9.3 %fusion.44 = bf16[12,128,1,6,64]{1,4,3,0,2:T(8,128)(2,1)} fusion(f32[12,6,128,128]{2,3,1,0:T(8,128)} %fusion.55, bf16[12,128,1,6,64]{1,4,3,0,2:T(8,128)(2,1)} %copy.67, f32[12,6,128,128]{2,3,1,0:T(8,128)} %copy-done.13, f32[12,6,128]{2,1,0:T(8,128)S(1)} %get-tuple-element.16), kind=kOutput, calls=%fused_computation.52 | convolution fusion | flops 159261824 | bytes 11833344 | tf_op jit(solution)/shard_map/nhqk,nqhe->nkhe/dot_general | solution.py:67
  185.9 9.4 %fusion.41 = bf16[12,128,1,6,64]{1,4,3,0,2:T(8,128)(2,1)} fusion(f32[12,6,128,128]{2,3,1,0:T(8,128)} %fusion.55, bf16[12,128,1,6,64]{1,4,3,0,2:T(8,128)(2,1)} %copy.68, f32[12,6,128,128]{2,3,1,0:T(8,128)} %copy-done.13, f32[12,6,128]{2,1,0:T(8,128)S(1)} %get-tuple-element.16), kind=kOutput, calls=%fused_computation.51 | convolution fusion | flops 159261824 | bytes 11833344 | tf_op jit(solution)/shard_map/nhqk,nkhe->nqhe/dot_general | solution.py:64
  195.3 2.1 copy.53
  197.4 3.2 fusion.47
  200.7 0.7 maximum_convert_fusion
  201.4 3.1 copy.52
  204.5 3.3 fusion.23
  207.7 2.8 pad_maximum_fusion
  210.5 0.0 all-reduce.3.cloned.1.call-update
  210.6 1.2 reshape.193
  211.8 5.1 %copy.50 = bf16[12,128,3,6,64]{1,4,3,2,0:T(8,128)(2,1)} copy(bf16[12,128,3,6,64]{1,4,3,0,2:T(8,128)(2,1)} %copy-done.1) | data formatting | bytes 7077888 | tf_op jit(solution)/shard_map/convert_element_type | solution.py:72
  216.9 5.2 %reshape.194 = bf16[768,1152,1]{1,0,2:T(8,128)(2,1)} reshape(bf16[256,3,1152]{2,1,0:T(4,128)(2,1)} %all-gather.3.cloned.1.call-done) | data formatting | bytes 3538944
  222.1 6.7 %multiply_reduce_fusion.1 = (f32[12,128]{1,0:T(8,128)S(1)}, f32[12,128]{1,0:T(8,128)S(1)}, f32[12,128,768]{2,1,0:T(8,128)S(1)}) fusion(f32[768]{0:T(1024)S(1)} %copy-done.12, f32[12,128]{1,0:T(8,128)S(1)} %get-tuple-element.9, f32[12,128]{1,0:T(8,128)S(1)} %get-tuple-element.12, bf16[1,12,128,768]{3,2,1,0:T(8,128)(2,1)S(1)} %copy-done, ...), kind=kOutput, calls=%fused_computation.34 | convolution fusion | flops 2726163456 | bytes 12413952 | tf_op jit(solution)/shard_map/dot_general | solution.py:78
  228.8 3.0 fusion.34
  231.8 3.4 fusion.39
  235.2 245.7 %all-reduce.3.cloned.1.call-done = f32[768,1536]{1,0:T(8,128)} async-done(((f32[768,1536]{1,0:T(8,128)}), f32[768,1536]{1,0:T(8,128)}) %all-reduce.3.cloned.1.call-update) | async-done | bytes 4718608
  480.9 1.5 constant_dynamic-slice_fusion
  482.4 1.4 dynamic-slice.2
  (30 shorter events, 0.1 us)
Async XLA Ops:
  7.2 18.2 %copy-start = (bf16[1,12,128,768]{3,2,1,0:T(8,128)(2,1)S(1)}, bf16[1,12,128,768]{3,2,1,0:T(8,128)(2,1)}, u32[]{:S(2)}) copy-start(bf16[1,12,128,768]{3,2,1,0:T(8,128)(2,1)} %param.6) | copy-start | bytes 7077892
  7.2 112.8 %all-gather.3.cloned.1.call-start = ((), (), s32[]{:S(2)}) async-start(), calls=%async_computation.1 | async-start | bytes 2368512 | tf_op jit(solution)/shard_map/all_gather | solution.py:94
  9.7 40.0 %all-to-all-start = ((bf16[256,3,384]{2,1,0:T(4,128)(2,1)}), bf16[256,3,384]{2,1,0:T(4,128)(2,1)S(1)}, u32[]{:S(2)}, u32[]{:S(2)}) async-start(bf16[256,3,384]{2,1,0:T(4,128)(2,1)} %stack.10), calls=%async_computation | async-start | bytes 1572864 | tf_op jit(solution)/shard_map/all_to_all | solution.py:12
  24.4 456.5 %all-reduce.3.cloned.1.call-start = ((), (), s32[]{:S(2)}) async-start(), calls=%async_computation.2 | async-start | bytes 9437184
  24.4 2.1 copy-start.2
  25.7 2.5 copy-start.12
  165.6 2.8 copy-start.5
  168.3 2.5 copy-start.13
  168.3 2.5 copy-start.4
  197.4 3.3 copy-start.7
  197.4 3.3 copy-start.8
  197.4 3.3 copy-start.9
  201.3 3.1 copy-start.1
  201.3 3.1 copy-start.6
  222.1 6.7 %copy-start.10 = (bf16[12,6,64,128]{3,2,1,0:T(8,128)(2,1)S(1)}, bf16[12,6,64,128]{3,2,1,0:T(8,128)(2,1)}, u32[]{:S(2)}) copy-start(bf16[12,6,64,128]{3,2,1,0:T(8,128)(2,1)} %convolution_convert_fusion.2) | copy-start | bytes 3538948
  222.1 6.7 %copy-start.11 = (bf16[768,384,1]{1,0,2:T(8,128)(2,1)S(1)}, bf16[768,384,1]{1,0,2:T(8,128)(2,1)}, u32[]{:S(2)}) copy-start(bf16[768,384,1]{1,0,2:T(8,128)(2,1)} %reshape.193) | copy-start | bytes 1769476
  228.8 3.0 copy-start.3
Sparse Core Ops, SparseCore 0:
  11.6 108.3 all-gather.2
  210.7 270.1 all-reduce.2
